TPU v7x, 32 devices: a whole 2x2x4 slice. The times are simulated.
32 devices in a mesh: dp: 8 (over y, x, core), mp: 4 (over z).
Axes of the slice: x: 2, y: 2, z: 4, core: 2. Of those that a mesh axis runs over, the one named last changes fastest.
Arguments:
- patches: bfloat16 [8192, 768], P('dp'), may hold values from -6 to 6
- attention_gain: bfloat16 [768], replicated, may hold values from 0.5 to 1.5
- query_weight: bfloat16 [768, 768], P(None, 'mp'), may hold values from -0.0390625 to 0.0390625
- key_weight: bfloat16 [768, 768], P(None, 'mp'), may hold values from -0.3125 to 0.3125
- value_weight: bfloat16 [768, 768], P(None, 'mp'), may hold values from -0.21875 to 0.21875
- output_weight: bfloat16 [768, 768], P('mp'), may hold values from -0.875 to 0.875
- feedforward_gain: bfloat16 [768], replicated, may hold values from 0.5 to 1.5
- gate_weight: bfloat16 [768, 2048], P(None, 'mp'), may hold values from -0.21875 to 0.21875
- up_weight: bfloat16 [768, 2048], P(None, 'mp'), may hold values from -0.21875 to 0.21875
- down_weight: bfloat16 [2048, 768], P('mp'), may hold values from -0.25 to 0.25
- cotangent: bfloat16 [8192, 768], P('dp'), may hold values from -6 to 6
- grid_extent: int32 [8, 2], P('dp'), may hold values from 16 to 32, as said below
Outputs:
- layer_output: bfloat16 [8192, 768], P('dp')
- input_grad: float32 [8192, 768], P('dp')
- attention_grad: float32 [768], P('dp')
- query_grad: float32 [768, 768], P('dp', 'mp')
- key_grad: float32 [768, 768], P('dp', 'mp')
- value_grad: float32 [768, 768], P('dp', 'mp')
- output_grad: float32 [768, 768], P('mp', 'dp')
- feedforward_grad: float32 [768], P('dp')
- gate_grad: float32 [768, 2048], P('dp', 'mp')
- up_grad: float32 [768, 2048], P('dp', 'mp')
- down_grad: float32 [2048, 768], P('mp', 'dp')
Inputs may be any that keep to these rules, and one draw needn't show every extreme that they name: `grid_extent`: chart 0 has all 32 rows and columns.
All inputs are finite; a program needn't handle non-finite values.
Results may differ from a plain program's by a relative error of at most 0.015.
Values may be sent and summed in bfloat16 or wider, within the bound.
A program may use at most 128 MiB of HBM per device.

v0:
```python
import jax
import jax.numpy as jnp
from jax import lax
from jax.sharding import PartitionSpec as P

HEAD = 64
epsilon = 1e-06
masked_score = -1000000000.0


def rms_scale(values, gain_vec):
    return (
        values * lax.rsqrt(jnp.mean(values * values, axis=-1, keepdims=True) + epsilon) * gain_vec
    )


def patch_valid(grid_extent, length):
    position = jnp.arange(length, dtype=jnp.int32)
    return position[None, :] < grid_extent[:, 0:1] * grid_extent[:, 1:2]


def query_blocks(length):
    block_rows = min(512, length)
    return (block_rows, jnp.arange(length // block_rows, dtype=jnp.int32) * block_rows)


def block_scores(query_block, keys_all, key_bias):
    scores = jnp.einsum("qhd,khd->hqk", query_block, keys_all, preferred_element_type=jnp.float32)
    return scores + key_bias


def attend_chart(chart_item):
    queries, keys_all, values_all, key_ok = chart_item
    block_rows, starts = query_blocks(queries.shape[0])
    key_bias = jnp.where(key_ok, 0.0, masked_score).astype(jnp.float32)

    def one_block(start):
        query_block = lax.dynamic_slice_in_dim(queries, start, block_rows, 0)
        scores = block_scores(query_block, keys_all, key_bias)
        highest = jnp.max(scores, axis=-1, keepdims=True)
        logsum = highest + jnp.log(jnp.sum(jnp.exp(scores - highest), axis=-1, keepdims=True))
        probs = jnp.exp(scores - logsum).astype(jnp.bfloat16)
        context = jnp.einsum("hqk,khd->qhd", probs, values_all, preferred_element_type=jnp.float32)
        return (context.astype(jnp.bfloat16), logsum)

    context, logsum = lax.map(one_block, starts)
    return (context.reshape(queries.shape), logsum)


def attend_back(chart_item):
    queries, keys_all, values_all, key_ok, logsum, context_back = chart_item
    block_rows, starts = query_blocks(queries.shape[0])
    key_bias = jnp.where(key_ok, 0.0, masked_score).astype(jnp.float32)

    def one_block(carry, block_item):
        key_total, value_total = carry
        start, block_logsum = block_item
        query_block = lax.dynamic_slice_in_dim(queries, start, block_rows, 0)
        grad_block = lax.dynamic_slice_in_dim(context_back, start, block_rows, 0)
        probs_full = jnp.exp(block_scores(query_block, keys_all, key_bias) - block_logsum)
        value_total = value_total + jnp.einsum(
            "hqk,qhd->khd",
            probs_full.astype(jnp.bfloat16),
            grad_block,
            preferred_element_type=jnp.float32,
        )
        probs_back = jnp.einsum(
            "qhd,khd->hqk", grad_block, values_all, preferred_element_type=jnp.float32
        )
        score_back = probs_full * (
            probs_back - jnp.sum(probs_full * probs_back, axis=-1, keepdims=True)
        )
        score_back = score_back.astype(jnp.bfloat16)
        query_part = jnp.einsum(
            "hqk,khd->qhd", score_back, keys_all, preferred_element_type=jnp.float32
        )
        key_total = key_total + jnp.einsum(
            "hqk,qhd->khd", score_back, query_block, preferred_element_type=jnp.float32
        )
        return ((key_total, value_total), query_part.astype(jnp.bfloat16))

    zeros_keys = jnp.zeros(keys_all.shape, jnp.float32)
    (key_total, value_total), query_back = lax.scan(
        one_block, (zeros_keys, zeros_keys), (starts, logsum)
    )
    return (
        query_back.reshape(queries.shape),
        key_total.astype(jnp.bfloat16),
        value_total.astype(jnp.bfloat16),
    )


def layer_forward(inputs, weights, valid_mask, attention_total):
    (
        first_gain,
        query_weight,
        key_weight,
        value_weight,
        output_weight,
        second_gain,
        gate_weight,
        up_weight,
        down_weight,
    ) = weights
    rows_total = inputs.shape[0]
    charts = valid_mask.shape[0]
    length = rows_total // charts
    normed_one = rms_scale(inputs, first_gain).astype(jnp.bfloat16)

    def project(matrix):
        product = jnp.dot(normed_one, matrix, preferred_element_type=jnp.float32)
        return product.astype(jnp.bfloat16).reshape(charts, length, matrix.shape[1] // HEAD, HEAD)

    queries = project(query_weight)
    keys_all = project(key_weight)
    values_all = project(value_weight)
    context, logsum = lax.map(attend_chart, (queries, keys_all, values_all, valid_mask))
    context = context.reshape(rows_total, query_weight.shape[1])
    attention_out = attention_total(
        jnp.dot(context, output_weight, preferred_element_type=jnp.float32)
    )
    hidden = inputs + attention_out
    normed_two = rms_scale(hidden, second_gain).astype(jnp.bfloat16)
    gate_pre = jnp.dot(normed_two, gate_weight, preferred_element_type=jnp.float32)
    up_pre = jnp.dot(normed_two, up_weight, preferred_element_type=jnp.float32)
    mixed = (jax.nn.gelu(gate_pre, approximate=True) * up_pre).astype(jnp.bfloat16)
    return (
        normed_one,
        queries,
        keys_all,
        values_all,
        logsum,
        context,
        hidden,
        normed_two,
        gate_pre,
        up_pre,
        mixed,
    )


def gelu_product(gate_pre, up_pre):
    return jax.nn.gelu(gate_pre, approximate=True) * up_pre


def body(
    patches,
    attention_gain,
    query_weight,
    key_weight,
    value_weight,
    output_weight,
    feedforward_gain,
    gate_weight,
    up_weight,
    down_weight,
    cotangent,
    grid_extent,
):
    rows_total = patches.shape[0]
    charts = grid_extent.shape[0]
    length = rows_total // charts
    valid_mask = patch_valid(grid_extent, length)
    row_keep = valid_mask.reshape(rows_total, 1)
    inputs = patches.astype(jnp.float32)
    first_gain = attention_gain.astype(jnp.float32)
    second_gain = feedforward_gain.astype(jnp.float32)
    weights = (
        first_gain,
        query_weight,
        key_weight,
        value_weight,
        output_weight,
        second_gain,
        gate_weight,
        up_weight,
        down_weight,
    )

    def attention_total(partial_value):
        share = lax.psum_scatter(partial_value, "mp", scatter_dimension=0, tiled=True)
        return lax.all_gather(share, "mp", axis=0, tiled=True)

    def attention_repeat(partial_value):
        share = lax.psum_scatter(partial_value, "mp", scatter_dimension=0, tiled=True)
        return lax.all_gather(share, "mp", axis=0, tiled=True)

    first_pass = layer_forward(inputs, weights, valid_mask, attention_total)
    feedforward_share = lax.psum_scatter(
        jnp.dot(first_pass[10], down_weight, preferred_element_type=jnp.float32),
        "mp",
        scatter_dimension=0,
        tiled=True,
    )
    rows_here = feedforward_share.shape[0]
    row_start = lax.axis_index("mp") * rows_here
    hidden_here = lax.dynamic_slice_in_dim(first_pass[6], row_start, rows_here, 0)
    keep_here = lax.dynamic_slice_in_dim(row_keep, row_start, rows_here, 0)
    output_here = jnp.where(keep_here, hidden_here + feedforward_share, 0.0).astype(jnp.bfloat16)
    layer_output = lax.all_gather(output_here, "mp", axis=0, tiled=True)
    saved = layer_forward(inputs, weights, valid_mask, attention_repeat)
    (
        normed_one,
        queries,
        keys_all,
        values_all,
        logsum,
        context,
        hidden,
        normed_two,
        gate_pre,
        up_pre,
        mixed,
    ) = saved
    out_back = jnp.where(row_keep, cotangent.astype(jnp.float32), 0.0)
    out_low = out_back.astype(jnp.bfloat16)
    down_grad = jnp.einsum("rf,rd->fd", mixed, out_low, preferred_element_type=jnp.float32)
    mixed_back = jnp.einsum("rd,fd->rf", out_low, down_weight, preferred_element_type=jnp.float32)
    _, gelu_pull = jax.vjp(gelu_product, gate_pre, up_pre)
    gate_back, up_back = gelu_pull(mixed_back)
    gate_back = gate_back.astype(jnp.bfloat16)
    up_back = up_back.astype(jnp.bfloat16)
    gate_grad = jnp.einsum("rd,rf->df", normed_two, gate_back, preferred_element_type=jnp.float32)
    up_grad = jnp.einsum("rd,rf->df", normed_two, up_back, preferred_element_type=jnp.float32)
    normed_two_part = jnp.einsum(
        "rf,df->rd", gate_back, gate_weight, preferred_element_type=jnp.float32
    ) + jnp.einsum("rf,df->rd", up_back, up_weight, preferred_element_type=jnp.float32)
    normed_two_share = lax.psum_scatter(normed_two_part, "mp", scatter_dimension=0, tiled=True)
    normed_two_back = lax.all_gather(normed_two_share, "mp", axis=0, tiled=True)
    _, second_pull = jax.vjp(rms_scale, hidden, second_gain)
    hidden_part, second_gain_grad = second_pull(normed_two_back)
    hidden_back = out_back + hidden_part
    second_gain_grad, gate_grad, up_grad = (
        lax.psum_scatter(second_gain_grad, "dp", scatter_dimension=0, tiled=True),
        lax.psum_scatter(gate_grad, "dp", scatter_dimension=0, tiled=True),
        lax.psum_scatter(up_grad, "dp", scatter_dimension=0, tiled=True),
    )
    down_grad = lax.psum_scatter(down_grad, "dp", scatter_dimension=1, tiled=True)
    hidden_low = hidden_back.astype(jnp.bfloat16)
    output_grad = jnp.einsum("rc,rd->cd", context, hidden_low, preferred_element_type=jnp.float32)
    context_back = jnp.einsum(
        "rd,cd->rc", hidden_low, output_weight, preferred_element_type=jnp.float32
    )
    context_back = context_back.astype(jnp.bfloat16).reshape(queries.shape)
    query_back, key_back, value_back = lax.map(
        attend_back, (queries, keys_all, values_all, valid_mask, logsum, context_back)
    )
    features_here = query_weight.shape[1]
    query_back = query_back.reshape(rows_total, features_here)
    key_back = key_back.reshape(rows_total, features_here)
    value_back = value_back.reshape(rows_total, features_here)
    query_grad = jnp.einsum("rd,rc->dc", normed_one, query_back, preferred_element_type=jnp.float32)
    key_grad = jnp.einsum("rd,rc->dc", normed_one, key_back, preferred_element_type=jnp.float32)
    value_grad = jnp.einsum("rd,rc->dc", normed_one, value_back, preferred_element_type=jnp.float32)
    normed_one_part = (
        jnp.einsum("rc,dc->rd", query_back, query_weight, preferred_element_type=jnp.float32)
        + jnp.einsum("rc,dc->rd", key_back, key_weight, preferred_element_type=jnp.float32)
        + jnp.einsum("rc,dc->rd", value_back, value_weight, preferred_element_type=jnp.float32)
    )
    normed_one_share = lax.psum_scatter(normed_one_part, "mp", scatter_dimension=0, tiled=True)
    normed_one_back = lax.all_gather(normed_one_share, "mp", axis=0, tiled=True)
    _, first_pull = jax.vjp(rms_scale, inputs, first_gain)
    input_part, first_gain_grad = first_pull(normed_one_back)
    input_grad = hidden_back + input_part
    first_gain_grad, query_grad, key_grad, value_grad = (
        lax.psum_scatter(first_gain_grad, "dp", scatter_dimension=0, tiled=True),
        lax.psum_scatter(query_grad, "dp", scatter_dimension=0, tiled=True),
        lax.psum_scatter(key_grad, "dp", scatter_dimension=0, tiled=True),
        lax.psum_scatter(value_grad, "dp", scatter_dimension=0, tiled=True),
    )
    output_grad = lax.psum_scatter(output_grad, "dp", scatter_dimension=1, tiled=True)
    return (
        layer_output,
        input_grad,
        first_gain_grad,
        query_grad,
        key_grad,
        value_grad,
        output_grad,
        second_gain_grad,
        gate_grad,
        up_grad,
        down_grad,
    )


def solution(mesh):
    placed = (
        P("dp", None),
        P(),
        P(None, "mp"),
        P(None, "mp"),
        P(None, "mp"),
        P("mp", None),
        P(),
        P(None, "mp"),
        P(None, "mp"),
        P("mp", None),
        P("dp", None),
        P("dp", None),
    )
    return jax.shard_map(
        body,
        mesh=mesh,
        in_specs=placed,
        out_specs=(
            P("dp", None),
            P("dp", None),
            P("dp"),
            P("dp", "mp"),
            P("dp", "mp"),
            P("dp", "mp"),
            P("mp", "dp"),
            P("dp"),
            P("dp", "mp"),
            P("dp", "mp"),
            P("mp", "dp"),
        ),
        check_vma=False,
    )
```

profile of v0, /device:TPU:0, one launch (start us, length us, event | category | flops | bytes accessed | tf_op | source)
XLA Modules:
  0.0 994.6 jit_solution(6283610246792495754)
XLA Ops:
  16.5 12.8 %while.67 = (s32[]{:T(128)}, bf16[2,512,3,64]{1,3,2,0:T(8,128)(2,1)S(1)}, f32[2,3,512,1]{2,1,3,0:T(4,128)S(1)}, s32[2]{0:T(128)S(1)}, bf16[1024,3,64]{0,2,1:T(8,...) while((s32[]{:T(128)}, ...), condition=%wide.region_11.12_spmd.clone, body=%wide.region_8.11_spmd.clone.sunk | while | flops 415334912 | bytes 20129972 | solution.py:46
  33.3 63.0 %reduce-scatter.19.cloned.1.call-done = f32[256,768]{1,0:T(8,128)} async-done(((f32[1024,768]{1,0:T(8,128)}), f32[256,768]{1,0:T(8,128)}) %reduce-scatter.19.cloned.1.call-update) | async-done | bytes 786448 | tf_op jit(solution)/shard_map/reduce_scatter | solution.py:185
  96.5 65.0 %all-gather.10.cloned.1.call-done = f32[1024,768]{1,0:T(8,128)} async-done(((f32[256,768]{1,0:T(8,128)}), f32[1024,768]{1,0:T(8,128)}) %all-gather.10.cloned.1.call-update) | async-done | bytes 3145744 | tf_op jit(solution)/shard_map/all_gather | solution.py:186
  169.1 2.8 multiply_convert_fusion.4
  173.1 2.7 convolution_add_fusion
  175.9 59.0 %reduce-scatter.21.cloned.1.call-done = f32[256,768]{1,0:T(8,128)} async-done(((f32[1024,768]{1,0:T(8,128)}), f32[256,768]{1,0:T(8,128)}) %reduce-scatter.21.cloned.1.call-update) | async-done | bytes 786448 | tf_op jit(solution)/shard_map/reduce_scatter | solution.py:228
  235.5 64.4 %all-gather.12.cloned.1.call-done = f32[1024,768]{1,0:T(8,128)} async-done(((f32[256,768]{1,0:T(8,128)}), f32[1024,768]{1,0:T(8,128)}) %all-gather.12.cloned.1.call-update) | async-done | bytes 3145744 | tf_op jit(solution)/shard_map/all_gather | solution.py:229
  300.0 4.6 multiply_reduce_fusion.1
  310.5 24.8 %while.68 = (s32[]{:T(128)}, f32[1024,3,64]{0,2,1:T(8,128)S(1)}, f32[1024,3,64]{0,2,1:T(8,128)}, bf16[2,512,3,64]{1,3,2,0:T(8,128)(2,1)}, s32[2]{0:T(128)}, /*in...) while((s32[]{:T(128)}, f32[1024,3,64]{0,2,1:T(8,128)S(1)}, ...), condition=%wide.region_18.19_spmd.clone, body=%wide.region_16.18_spmd.clone.sunk | while | flops 1026392576 | bytes 66714016 | solution.py:83
  342.1 14.3 %while.66 = (s32[]{:T(128)}, bf16[2,512,3,64]{1,3,2,0:T(8,128)(2,1)}, s32[2]{0:T(128)S(1)}, bf16[1024,3,64]{0,2,1:T(8,128)(2,1)S(1)}, bf16[1024,3,64]{0,2,1:T(8,...) while((s32[]{:T(128)}, ...), condition=%wide.region_4.5_spmd.clone, body=%wide.region_1.4_spmd.clone.sunk | while | flops 415334912 | bytes 23261408 | solution.py:46
  357.9 3.3 fusion.97
  361.2 38.9 %reduce-scatter.23.cloned.1.call-done = f32[256,768]{1,0:T(8,128)} async-done(((f32[1024,768]{1,0:T(8,128)}), f32[256,768]{1,0:T(8,128)}) %reduce-scatter.23.cloned.1.call-update) | async-done | bytes 786448 | tf_op jit(solution)/shard_map/reduce_scatter | solution.py:260
  400.2 63.0 %reduce-scatter.15.cloned.1.call-done = f32[256,768]{1,0:T(8,128)} async-done(((f32[1024,768]{1,0:T(8,128)}), f32[256,768]{1,0:T(8,128)}) %reduce-scatter.15.cloned.1.call-update) | async-done | bytes 786448 | tf_op jit(solution)/shard_map/reduce_scatter | solution.py:181
  463.2 65.1 %all-gather.14.cloned.1.call-done = f32[1024,768]{1,0:T(8,128)} async-done(((f32[256,768]{1,0:T(8,128)}), f32[1024,768]{1,0:T(8,128)}) %all-gather.14.cloned.1.call-update) | async-done | bytes 3145744 | tf_op jit(solution)/shard_map/all_gather | solution.py:261
  528.3 3.0 fusion.50
  531.3 60.7 %all-gather.6.cloned.1.call-done = f32[1024,768]{1,0:T(8,128)} async-done(((f32[256,768]{1,0:T(8,128)}), f32[1024,768]{1,0:T(8,128)}) %all-gather.6.cloned.1.call-update) | async-done | bytes 3145744 | tf_op jit(solution)/shard_map/all_gather | solution.py:182
  592.0 5.6 multiply_reduce_fusion.4
  601.7 6.3 fusion.72
  609.0 3.5 convolution_bitcast_fusion.1
  612.6 54.5 %reduce-scatter.17.cloned.1.call-done = f32[256,768]{1,0:T(8,128)} async-done(((f32[1024,768]{1,0:T(8,128)}), f32[256,768]{1,0:T(8,128)}) %reduce-scatter.17.cloned.1.call-update) | async-done | bytes 786448 | tf_op jit(solution)/shard_map/reduce_scatter | solution.py:189
  669.6 5.5 fusion.73
  675.2 3.4 fusion.107
  678.7 4.1 fusion.108
  688.8 16.3 %reduce-scatter.37.cloned.1.call-done = f32[96,192]{1,0:T(8,128)} async-done(((f32[768,192]{1,0:T(8,128)}), f32[96,192]{1,0:T(8,128)}) %reduce-scatter.37.cloned.1.call-update) | async-done | bytes 73744
  706.7 12.6 %all-reduce.2 = (f32[768]{0:T(1024)S(1)}, f32[768]{0:T(1024)S(1)}) all-reduce(f32[768]{0:T(1024)S(1)} %get-tuple-element.302, f32[768]{0:T(1024)S(1)} %copy-done.60), channel_id=7, replica_groups=mesh['dp'=8,'mp'=4] {'dp'}, use_global_device_ids=true, to_apply=%region_22.23.clone | all-reduce | flops 1536 | bytes 12288
  720.5 23.3 %all-gather.8.cloned.1.call-done = bf16[1024,768]{1,0:T(8,128)(2,1)} async-done(((bf16[256,768]{1,0:T(8,128)(2,1)}), bf16[1024,768]{1,0:T(8,128)(2,1)}) %all-gather.8.cloned.1.call-update) | async-done | bytes 1572880 | tf_op jit(solution)/shard_map/all_gather | solution.py:200
  743.8 41.1 %reduce-scatter.35.cloned.1.call-done = f32[512,96]{0,1:T(8,128)} async-done(((f32[512,768]{0,1:T(8,128)}), f32[512,96]{0,1:T(8,128)}) %reduce-scatter.35.cloned.1.call-update) | async-done | bytes 196624 | tf_op jit(solution)/shard_map/reduce_scatter | solution.py:238
  784.9 42.4 %reduce-scatter.31.cloned.1.call-done = f32[96,512]{1,0:T(8,128)} async-done(((f32[768,512]{1,0:T(8,128)}), f32[96,512]{1,0:T(8,128)}) %reduce-scatter.31.cloned.1.call-update) | async-done | bytes 196624 | tf_op jit(solution)/shard_map/reduce_scatter | solution.py:235
  827.2 42.2 %reduce-scatter.33.cloned.1.call-done = f32[96,512]{1,0:T(8,128)} async-done(((f32[768,512]{1,0:T(8,128)}), f32[96,512]{1,0:T(8,128)}) %reduce-scatter.33.cloned.1.call-update) | async-done | bytes 196624 | tf_op jit(solution)/shard_map/reduce_scatter | solution.py:236
  869.5 38.6 %reduce-scatter.29.cloned.1.call-done = f32[96,192]{1,0:T(8,128)} async-done(((f32[768,192]{1,0:T(8,128)}), f32[96,192]{1,0:T(8,128)}) %reduce-scatter.29.cloned.1.call-update) | async-done | bytes 73744 | tf_op jit(solution)/shard_map/reduce_scatter | solution.py:269
  908.0 38.6 %reduce-scatter.25.cloned.1.call-done = f32[96,192]{1,0:T(8,128)} async-done(((f32[768,192]{1,0:T(8,128)}), f32[96,192]{1,0:T(8,128)}) %reduce-scatter.25.cloned.1.call-update) | async-done | bytes 73744 | tf_op jit(solution)/shard_map/reduce_scatter | solution.py:267
  946.6 38.6 %reduce-scatter.27.cloned.1.call-done = f32[96,192]{1,0:T(8,128)} async-done(((f32[768,192]{1,0:T(8,128)}), f32[96,192]{1,0:T(8,128)}) %reduce-scatter.27.cloned.1.call-update) | async-done | bytes 73744 | tf_op jit(solution)/shard_map/reduce_scatter | solution.py:268
  (289 shorter events, 93.6 us)
Async XLA Ops:
  7.2 159.5 %copy-start = (bf16[768,512]{1,0:T(8,128)(2,1)S(1)}, bf16[768,512]{1,0:T(8,128)(2,1)}, u32[]{:S(2)}) copy-start(bf16[768,512]{1,0:T(8,128)(2,1)} %param.26) | copy-start | bytes 2359300
  7.2 5.9 copy-start.41
  7.2 89.2 %reduce-scatter.19.cloned.1.call-start = ((), (), s32[]{:S(2)}) async-start(), calls=%async_computation.16 | async-start | bytes 3932160 | tf_op jit(solution)/shard_map/reduce_scatter | solution.py:185
  16.5 14.5 %copy-start.29 = (bf16[192,768]{1,0:T(8,128)(2,1)S(1)}, bf16[192,768]{1,0:T(8,128)(2,1)}, u32[]{:S(2)}) copy-start(bf16[192,768]{1,0:T(8,128)(2,1)} %param.23) | copy-start | bytes 884740
  31.0 65.5 %copy-start.61 = (bf16[768]{0:T(1024)(128)(2,1)S(1)}, bf16[768]{0:T(1024)(128)(2,1)}, u32[]{:S(2)}) copy-start(bf16[768]{0:T(1024)(128)(2,1)} %param.24) | copy-start | bytes 4612
  31.0 130.6 %copy-start.1 = (bf16[1024,768]{1,0:T(8,128)(2,1)S(1)}, bf16[1024,768]{1,0:T(8,128)(2,1)}, u32[]{:S(2)}) copy-start(bf16[1024,768]{1,0:T(8,128)(2,1)} %param.18) | copy-start | bytes 4718596
  33.3 128.2 %all-gather.10.cloned.1.call-start = ((), (), s32[]{:S(2)}) async-start(), calls=%async_computation.17 | async-start | bytes 3932160 | tf_op jit(solution)/shard_map/all_gather | solution.py:186
  96.4 138.5 %reduce-scatter.21.cloned.1.call-start = ((), (), s32[]{:S(2)}) async-start(), calls=%async_computation.18 | async-start | bytes 3932160 | tf_op jit(solution)/shard_map/reduce_scatter | solution.py:228
  96.5 68.4 %copy-start.47 = (f32[768]{0:T(1024)}, f32[768]{0:T(1024)S(1)}, u32[]{:S(2)}) copy-start(f32[768]{0:T(1024)S(1)} %convert_element_type.102) | copy-start | bytes 9220
  96.5 71.2 %copy-start.62 = (pred[1024]{0:T(1024)(128)(4,1)}, pred[1024]{0:T(1024)(128)(4,1)S(1)}, u32[]{:S(2)}) copy-start(pred[1024]{0:T(1024)(128)(4,1)S(1)} %iota_compare_fusion.3) | copy-start | bytes 3076
  175.9 124.0 %all-gather.12.cloned.1.call-start = ((), (), s32[]{:S(2)}) async-start(), calls=%async_computation.19 | async-start | bytes 3932160 | tf_op jit(solution)/shard_map/all_gather | solution.py:229
  235.0 165.2 %reduce-scatter.23.cloned.1.call-start = ((), (), s32[]{:S(2)}) async-start(), calls=%async_computation.20 | async-start | bytes 3932160 | tf_op jit(solution)/shard_map/reduce_scatter | solution.py:260
  341.1 122.1 %reduce-scatter.15.cloned.1.call-start = ((), (), s32[]{:S(2)}) async-start(), calls=%async_computation.12 | async-start | bytes 3932160 | tf_op jit(solution)/shard_map/reduce_scatter | solution.py:181
  361.1 167.2 %copy-start.51 = (f32[768]{0:T(1024)S(1)}, f32[768]{0:T(1024)}, u32[]{:S(2)}) copy-start(f32[768]{0:T(1024)} %copy-done.50) | copy-start | bytes 9220
  361.1 167.2 %copy-start.53 = (f32[1024]{0:T(1024)S(1)}, f32[1024]{0:T(1024)}, u32[]{:S(2)}) copy-start(f32[1024]{0:T(1024)} %copy-done.52) | copy-start | bytes 12292
  361.2 167.1 %all-gather.14.cloned.1.call-start = ((), (), s32[]{:S(2)}) async-start(), calls=%async_computation.21 | async-start | bytes 3932160 | tf_op jit(solution)/shard_map/all_gather | solution.py:261
  400.1 131.2 %copy-start.57 = (f32[1024]{0:T(1024)S(1)}, f32[1024]{0:T(1024)}, u32[]{:S(2)}) copy-start(f32[1024]{0:T(1024)} %copy-done.56) | copy-start | bytes 12292
  400.1 191.9 %all-gather.6.cloned.1.call-start = ((), (), s32[]{:S(2)}) async-start(), calls=%async_computation.13 | async-start | bytes 3932160 | tf_op jit(solution)/shard_map/all_gather | solution.py:182
  463.2 203.9 %reduce-scatter.17.cloned.1.call-start = ((), (), s32[]{:S(2)}) async-start(), calls=%async_computation.14 | async-start | bytes 3932160 | tf_op jit(solution)/shard_map/reduce_scatter | solution.py:189
  531.3 68.0 %copy-start.28 = (bf16[768,512]{1,0:T(8,128)(2,1)S(1)}, bf16[768,512]{1,0:T(8,128)(2,1)}, u32[]{:S(2)}) copy-start(bf16[768,512]{1,0:T(8,128)(2,1)} %param.25) | copy-start | bytes 2359300
  531.3 68.0 %copy-start.49 = (f32[768]{0:T(1024)S(1)}, f32[768]{0:T(1024)}, u32[]{:S(2)}) copy-start(f32[768]{0:T(1024)} %copy-done.47) | copy-start | bytes 9220
  608.0 61.6 %copy-start.64 = (pred[1024]{0:T(1024)(128)(4,1)S(1)}, pred[1024]{0:T(1024)(128)(4,1)}, u32[]{:S(2)}) copy-start(pred[1024]{0:T(1024)(128)(4,1)} %copy-done.62) | copy-start | bytes 3076
  608.0 97.1 %reduce-scatter.37.cloned.1.call-start = ((), (), s32[]{:S(2)}) async-start(), calls=%async_computation.28 | async-start | bytes 884736
  612.5 131.3 %all-gather.8.cloned.1.call-start = ((), (), s32[]{:S(2)}) async-start(), calls=%async_computation.15 | async-start | bytes 1966080 | tf_op jit(solution)/shard_map/all_gather | solution.py:200
  669.3 5.9 copy-start.36
  669.3 115.6 %reduce-scatter.35.cloned.1.call-start = ((), (), s32[]{:S(2)}) async-start(), calls=%async_computation.27 | async-start | bytes 1769472 | tf_op jit(solution)/shard_map/reduce_scatter | solution.py:238
  675.1 152.1 %reduce-scatter.31.cloned.1.call-start = ((), (), s32[]{:S(2)}) async-start(), calls=%async_computation.25 | async-start | bytes 1769472 | tf_op jit(solution)/shard_map/reduce_scatter | solution.py:235
  678.6 190.8 %reduce-scatter.33.cloned.1.call-start = ((), (), s32[]{:S(2)}) async-start(), calls=%async_computation.26 | async-start | bytes 1769472 | tf_op jit(solution)/shard_map/reduce_scatter | solution.py:236
  682.8 225.3 %reduce-scatter.29.cloned.1.call-start = ((), (), s32[]{:S(2)}) async-start(), calls=%async_computation.24 | async-start | bytes 884736 | tf_op jit(solution)/shard_map/reduce_scatter | solution.py:269
  684.4 22.4 %copy-start.60 = (f32[768]{0:T(1024)S(1)}, f32[768]{0:T(1024)}, u32[]{:S(2)}) copy-start(f32[768]{0:T(1024)} %get-tuple-element.300) | copy-start | bytes 9220
  684.4 262.2 %reduce-scatter.25.cloned.1.call-start = ((), (), s32[]{:S(2)}) async-start(), calls=%async_computation.22 | async-start | bytes 884736 | tf_op jit(solution)/shard_map/reduce_scatter | solution.py:267
  686.0 299.3 %reduce-scatter.27.cloned.1.call-start = ((), (), s32[]{:S(2)}) async-start(), calls=%async_computation.23 | async-start | bytes 884736 | tf_op jit(solution)/shard_map/reduce_scatter | solution.py:268
  (66 other events, 141.5 us)
Sparse Core Ops, SparseCore 0:
  33.4 62.9 reduce-scatter.18
  98.0 63.5 all-gather.9
  176.0 58.8 reduce-scatter.20
  236.4 63.5 all-gather.11
  341.2 58.8 reduce-scatter.22
  402.8 60.2 reduce-scatter.14
  464.7 63.5 all-gather.13
  529.9 62.1 all-gather.5
  608.1 58.8 reduce-scatter.16
  670.0 35.0 reduce-scatter.36
  706.7 37.0 all-gather.7
  747.5 37.3 reduce-scatter.34
  788.7 38.4 reduce-scatter.30
  831.0 38.4 reduce-scatter.32
  873.0 34.9 reduce-scatter.28
  911.6 34.9 reduce-scatter.24
  950.2 34.9 reduce-scatter.26
where the time goes:
time: 1000 us; the launch traced here: 995 us
  waiting for transfers between devices  815 us (82%)
  matrix products  75.7 us (8%)
  other arithmetic  32.9 us (3%)
  local copies, waits for them, and re-layouts  28 us (3%)
  between operations  16.9 us (2%)
  blocking collectives  12.6 us (1%)
  loops' own time  12.1 us (1%)
    all_gather x1, waiting for transfers between devices, body(): normed_one_back = lax.all_gather(normed_one_share, 'mp', axis=0, tiled=True)  65.1 us
    all_gather x1, waiting for transfers between devices, attention_repeat(): return lax.all_gather(share, 'mp', axis=0, tiled=True)  65 us
    all_gather x1, waiting for transfers between devices, body(): normed_two_back = lax.all_gather(normed_two_share, 'mp', axis=0, tiled=True)  64.4 us
    reduce_scatter x1, waiting for transfers between devices, attention_repeat(): lax.psum_scatter(partial_value, 'mp', scatter_dimension=0, tiled=True)  63 us
    reduce_scatter x1, waiting for transfers between devices, attention_total(): lax.psum_scatter(partial_value, 'mp', scatter_dimension=0, tiled=True)  63 us
    all_gather x1, waiting for transfers between devices, attention_total(): return lax.all_gather(share, 'mp', axis=0, tiled=True)  60.7 us
    reduce_scatter x1, waiting for transfers between devices, body(): lax.psum_scatter(normed_two_part, 'mp', scatter_dimension=0, tiled=True)  59 us
    reduce_scatter x1, waiting for transfers between devices, body(): lax.psum_scatter(jnp.dot(first_pass[10], down_weight, preferred_element_t...  54.5 us
  transfers between devices with their start and end apart: 17, of which 17 were waited for; matrix products, arithmetic and copies ran while one was open for 4% of the time, Pallas kernels for 0%

commit v1 on v0

--- a/solution.py
+++ b/solution.py
@@ -6,6 +6,23 @@
 HEAD = 64
 epsilon = 1e-06
 masked_score = -1000000000.0
+
+
+def digits_expand(local_values, across):
+    extent = lax.axis_size(across)
+    xs_all = []
+    for at in range(extent):
+        xs_all.append((at, (at + 1) % extent))
+    pool = []
+    for at in range(extent):
+        pool.append((at, (at - 1) % extent))
+    state_now, val = ([local_values], [local_values])
+    for _ in range(extent // 2):
+        state_now.append(lax.ppermute(state_now[-1], across, xs_all))
+    for _ in range((extent - 1) // 2):
+        val.append(lax.ppermute(val[-1], across, pool))
+    near = jnp.concatenate([*state_now[::-1], *val[1:]], 0)
+    return jnp.roll(near, (lax.axis_index(across) - extent // 2) * local_values.shape[0], axis=0)
 
 
 def rms_scale(values, gain_vec):
@@ -197,7 +214,7 @@
     hidden_here = lax.dynamic_slice_in_dim(first_pass[6], row_start, rows_here, 0)
     keep_here = lax.dynamic_slice_in_dim(row_keep, row_start, rows_here, 0)
     output_here = jnp.where(keep_here, hidden_here + feedforward_share, 0.0).astype(jnp.bfloat16)
-    layer_output = lax.all_gather(output_here, "mp", axis=0, tiled=True)
+    layer_output = digits_expand(output_here, "mp")
     saved = layer_forward(inputs, weights, valid_mask, attention_repeat)
     (
         normed_one,

time: 1000 us -> 964 us (0.964)
  waiting for transfers between devices: 815 us -> 769 us
    all_gather x1 -> x0, waiting for transfers between devices: 23.3 us -> none  [body(): layer_output = lax.all_gather(output_here, 'mp', axis=0, tiled=True)]
    reduce_scatter x1, waiting for transfers between devices: 41.1 us -> 21.4 us  [body(): lax.psum_scatter(down_grad, 'dp', scatter_dimension=1, tiled=True)]
    reduce_scatter x1, waiting for transfers between devices: 54.5 us -> 38.9 us  [body(): lax.psum_scatter(jnp.dot(first_pass[10], down_weight, preferred_element_t...]
    ppermute x0 -> x3, waiting for transfers between devices: none -> 11.5 us  [the longest x2 11.5 us: digits_expand(): state_now.append(lax.ppermute(state_now[-1], across, xs_all))]
  transfers between devices with their start and end apart: 17 -> 19, of which waited for: 17 -> 17; matrix products, arithmetic and copies ran while one was open for 4% -> 5% of each run, Pallas kernels for 0% -> 0%
where the time goes in v1:
time: 964 us; the launch traced here: 955 us
  waiting for transfers between devices  769 us (80%)
  matrix products  74.5 us (8%)
  other arithmetic  32.1 us (3%)
  local copies, waits for them, and re-layouts  31.1 us (3%)
  between operations  16.9 us (2%)
  blocking collectives  12.6 us (1%)
  loops' own time  12.1 us (1%)
    all_gather x1, waiting for transfers between devices, body(): normed_one_back = lax.all_gather(normed_one_share, 'mp', axis=0, tiled=True)  65 us
    all_gather x1, waiting for transfers between devices, attention_repeat(): return lax.all_gather(share, 'mp', axis=0, tiled=True)  65 us
    all_gather x1, waiting for transfers between devices, body(): normed_two_back = lax.all_gather(normed_two_share, 'mp', axis=0, tiled=True)  64.4 us
    reduce_scatter x1, waiting for transfers between devices, attention_repeat(): lax.psum_scatter(partial_value, 'mp', scatter_dimension=0, tiled=True)  63 us
    reduce_scatter x1, waiting for transfers between devices, attention_total(): lax.psum_scatter(partial_value, 'mp', scatter_dimension=0, tiled=True)  63 us
    all_gather x1, waiting for transfers between devices, attention_total(): return lax.all_gather(share, 'mp', axis=0, tiled=True)  60.7 us
    reduce_scatter x1, waiting for transfers between devices, body(): lax.psum_scatter(normed_two_part, 'mp', scatter_dimension=0, tiled=True)  59 us
    reduce_scatter x1, waiting for transfers between devices, body(): lax.psum_scatter(up_grad, 'dp', scatter_dimension=0, tiled=True)  42.4 us
  transfers between devices with their start and end apart: 19, of which 17 were waited for; matrix products, arithmetic and copies ran while one was open for 5% of the time, Pallas kernels for 0%

profile of v1, /device:TPU:0, one launch (start us, length us, event | category | flops | bytes accessed | tf_op | source)
XLA Modules:
  0.0 954.8 jit_solution(10973841947188669912)
XLA Ops:
  16.5 12.8 %while.67 = (s32[]{:T(128)}, bf16[2,512,3,64]{1,3,2,0:T(8,128)(2,1)S(1)}, f32[2,3,512,1]{2,1,3,0:T(4,128)S(1)}, s32[2]{0:T(128)S(1)}, bf16[1024,3,64]{0,2,1:T(8,...) while((s32[]{:T(128)}, ...), condition=%wide.region_11.12_spmd.clone, body=%wide.region_8.11_spmd.clone.sunk | while | flops 415334912 | bytes 20129972 | solution.py:63
  33.5 63.0 %reduce-scatter.19.cloned.1.call-done = f32[256,768]{1,0:T(8,128)} async-done(((f32[1024,768]{1,0:T(8,128)}), f32[256,768]{1,0:T(8,128)}) %reduce-scatter.19.cloned.1.call-update) | async-done | bytes 786448 | tf_op jit(solution)/shard_map/reduce_scatter | solution.py:202
  96.7 65.0 %all-gather.7.cloned.1.call-done = f32[1024,768]{1,0:T(8,128)} async-done(((f32[256,768]{1,0:T(8,128)}), f32[1024,768]{1,0:T(8,128)}) %all-gather.7.cloned.1.call-update) | async-done | bytes 3145744 | tf_op jit(solution)/shard_map/all_gather | solution.py:203
  169.2 2.8 multiply_convert_fusion.4
  173.4 2.7 convolution_add_fusion
  176.2 59.0 %reduce-scatter.21.cloned.1.call-done = f32[256,768]{1,0:T(8,128)} async-done(((f32[1024,768]{1,0:T(8,128)}), f32[256,768]{1,0:T(8,128)}) %reduce-scatter.21.cloned.1.call-update) | async-done | bytes 786448 | tf_op jit(solution)/shard_map/reduce_scatter | solution.py:245
  235.8 64.4 %all-gather.9.cloned.1.call-done = f32[1024,768]{1,0:T(8,128)} async-done(((f32[256,768]{1,0:T(8,128)}), f32[1024,768]{1,0:T(8,128)}) %all-gather.9.cloned.1.call-update) | async-done | bytes 3145744 | tf_op jit(solution)/shard_map/all_gather | solution.py:246
  300.3 4.6 multiply_reduce_fusion.1
  310.8 24.9 %while.68 = (s32[]{:T(128)}, f32[1024,3,64]{0,2,1:T(8,128)S(1)}, f32[1024,3,64]{0,2,1:T(8,128)}, bf16[2,512,3,64]{1,3,2,0:T(8,128)(2,1)}, s32[2]{0:T(128)}, /*in...) while((s32[]{:T(128)}, f32[1024,3,64]{0,2,1:T(8,128)S(1)}, ...), condition=%wide.region_18.19_spmd.clone, body=%wide.region_16.18_spmd.clone.sunk | while | flops 1026392576 | bytes 66714016 | solution.py:100
  342.4 14.3 %while.66 = (s32[]{:T(128)}, bf16[2,512,3,64]{1,3,2,0:T(8,128)(2,1)}, s32[2]{0:T(128)S(1)}, bf16[1024,3,64]{0,2,1:T(8,128)(2,1)S(1)}, bf16[1024,3,64]{0,2,1:T(8,...) while((s32[]{:T(128)}, ...), condition=%wide.region_4.5_spmd.clone, body=%wide.region_1.4_spmd.clone.sunk | while | flops 415334912 | bytes 23261408 | solution.py:63
  358.2 3.3 fusion.97
  361.5 38.9 %reduce-scatter.23.cloned.1.call-done = f32[256,768]{1,0:T(8,128)} async-done(((f32[1024,768]{1,0:T(8,128)}), f32[256,768]{1,0:T(8,128)}) %reduce-scatter.23.cloned.1.call-update) | async-done | bytes 786448 | tf_op jit(solution)/shard_map/reduce_scatter | solution.py:277
  400.5 63.0 %reduce-scatter.15.cloned.1.call-done = f32[256,768]{1,0:T(8,128)} async-done(((f32[1024,768]{1,0:T(8,128)}), f32[256,768]{1,0:T(8,128)}) %reduce-scatter.15.cloned.1.call-update) | async-done | bytes 786448 | tf_op jit(solution)/shard_map/reduce_scatter | solution.py:198
  463.5 65.0 %all-gather.11.cloned.1.call-done = f32[1024,768]{1,0:T(8,128)} async-done(((f32[256,768]{1,0:T(8,128)}), f32[1024,768]{1,0:T(8,128)}) %all-gather.11.cloned.1.call-update) | async-done | bytes 3145744 | tf_op jit(solution)/shard_map/all_gather | solution.py:278
  528.6 3.0 fusion.50
  531.6 60.7 %all-gather.5.cloned.1.call-done = f32[1024,768]{1,0:T(8,128)} async-done(((f32[256,768]{1,0:T(8,128)}), f32[1024,768]{1,0:T(8,128)}) %all-gather.5.cloned.1.call-update) | async-done | bytes 3145744 | tf_op jit(solution)/shard_map/all_gather | solution.py:199
  592.3 5.6 multiply_reduce_fusion.4
  601.9 6.2 fusion.72
  609.2 3.6 convolution_bitcast_fusion.1
  612.8 5.6 fusion.73
  621.0 4.0 fusion.108
  628.3 38.9 %reduce-scatter.17.cloned.1.call-done = f32[256,768]{1,0:T(8,128)} async-done(((f32[1024,768]{1,0:T(8,128)}), f32[256,768]{1,0:T(8,128)}) %reduce-scatter.17.cloned.1.call-update) | async-done | bytes 786448 | tf_op jit(solution)/shard_map/reduce_scatter | solution.py:206
  669.8 11.5 %collective-permute-done = bf16[256,768]{1,0:T(8,128)(2,1)S(1)} collective-permute-done((bf16[256,768]{1,0:T(8,128)(2,1)S(1)}, bf16[256,768]{1,0:T(8,128)(2,1)S(1)}, u32[]{:S(2)}, u32[]{:S(2)}) %collective-permute-start) | collective-permute-done | bytes 393248 | tf_op jit(solution)/shard_map/ppermute | solution.py:21
  682.5 3.9 collective-permute-start.2
  687.9 17.4 %reduce-scatter.37.cloned.1.call-done = f32[96,192]{1,0:T(8,128)} async-done(((f32[768,192]{1,0:T(8,128)}), f32[96,192]{1,0:T(8,128)}) %reduce-scatter.37.cloned.1.call-update) | async-done | bytes 73744
  706.9 12.6 %all-reduce.2 = (f32[768]{0:T(1024)S(1)}, f32[768]{0:T(1024)S(1)}) all-reduce(f32[768]{0:T(1024)S(1)} %get-tuple-element.302, f32[768]{0:T(1024)S(1)} %copy-done.61), channel_id=7, replica_groups=mesh['dp'=8,'mp'=4] {'dp'}, use_global_device_ids=true, to_apply=%region_22.23.clone | all-reduce | flops 1536 | bytes 12288
  726.2 21.4 %reduce-scatter.35.cloned.1.call-done = f32[512,96]{0,1:T(8,128)} async-done(((f32[512,768]{0,1:T(8,128)}), f32[512,96]{0,1:T(8,128)}) %reduce-scatter.35.cloned.1.call-update) | async-done | bytes 196624 | tf_op jit(solution)/shard_map/reduce_scatter | solution.py:255
  747.7 42.2 %reduce-scatter.31.cloned.1.call-done = f32[96,512]{1,0:T(8,128)} async-done(((f32[768,512]{1,0:T(8,128)}), f32[96,512]{1,0:T(8,128)}) %reduce-scatter.31.cloned.1.call-update) | async-done | bytes 196624 | tf_op jit(solution)/shard_map/reduce_scatter | solution.py:252
  789.9 42.4 %reduce-scatter.33.cloned.1.call-done = f32[96,512]{1,0:T(8,128)} async-done(((f32[768,512]{1,0:T(8,128)}), f32[96,512]{1,0:T(8,128)}) %reduce-scatter.33.cloned.1.call-update) | async-done | bytes 196624 | tf_op jit(solution)/shard_map/reduce_scatter | solution.py:253
  832.3 38.6 %reduce-scatter.29.cloned.1.call-done = f32[96,192]{1,0:T(8,128)} async-done(((f32[768,192]{1,0:T(8,128)}), f32[96,192]{1,0:T(8,128)}) %reduce-scatter.29.cloned.1.call-update) | async-done | bytes 73744 | tf_op jit(solution)/shard_map/reduce_scatter | solution.py:286
  870.8 38.6 %reduce-scatter.25.cloned.1.call-done = f32[96,192]{1,0:T(8,128)} async-done(((f32[768,192]{1,0:T(8,128)}), f32[96,192]{1,0:T(8,128)}) %reduce-scatter.25.cloned.1.call-update) | async-done | bytes 73744 | tf_op jit(solution)/shard_map/reduce_scatter | solution.py:284
  909.4 38.6 %reduce-scatter.27.cloned.1.call-done = f32[96,192]{1,0:T(8,128)} async-done(((f32[768,192]{1,0:T(8,128)}), f32[96,192]{1,0:T(8,128)}) %reduce-scatter.27.cloned.1.call-update) | async-done | bytes 73744 | tf_op jit(solution)/shard_map/reduce_scatter | solution.py:285
  (302 shorter events, 99.2 us)
Async XLA Ops:
  7.2 159.6 %copy-start = (bf16[768,512]{1,0:T(8,128)(2,1)S(1)}, bf16[768,512]{1,0:T(8,128)(2,1)}, u32[]{:S(2)}) copy-start(bf16[768,512]{1,0:T(8,128)(2,1)} %param.26) | copy-start | bytes 2359300
  7.2 89.3 %reduce-scatter.19.cloned.1.call-start = ((), (), s32[]{:S(2)}) async-start(), calls=%async_computation.15 | async-start | bytes 3932160 | tf_op jit(solution)/shard_map/reduce_scatter | solution.py:202
  31.1 65.5 %copy-start.62 = (bf16[768]{0:T(1024)(128)(2,1)S(1)}, bf16[768]{0:T(1024)(128)(2,1)}, u32[]{:S(2)}) copy-start(bf16[768]{0:T(1024)(128)(2,1)} %param.24) | copy-start | bytes 4612
  31.1 130.6 %copy-start.1 = (bf16[1024,768]{1,0:T(8,128)(2,1)S(1)}, bf16[1024,768]{1,0:T(8,128)(2,1)}, u32[]{:S(2)}) copy-start(bf16[1024,768]{1,0:T(8,128)(2,1)} %param.18) | copy-start | bytes 4718596
  33.4 128.2 %all-gather.7.cloned.1.call-start = ((), (), s32[]{:S(2)}) async-start(), calls=%async_computation.16 | async-start | bytes 3932160 | tf_op jit(solution)/shard_map/all_gather | solution.py:203
  96.6 138.7 %reduce-scatter.21.cloned.1.call-start = ((), (), s32[]{:S(2)}) async-start(), calls=%async_computation.17 | async-start | bytes 3932160 | tf_op jit(solution)/shard_map/reduce_scatter | solution.py:245
  96.6 68.4 %copy-start.48 = (f32[768]{0:T(1024)}, f32[768]{0:T(1024)S(1)}, u32[]{:S(2)}) copy-start(f32[768]{0:T(1024)S(1)} %convert_element_type.102) | copy-start | bytes 9220
  96.6 71.2 %copy-start.63 = (pred[1024]{0:T(1024)(128)(4,1)}, pred[1024]{0:T(1024)(128)(4,1)S(1)}, u32[]{:S(2)}) copy-start(pred[1024]{0:T(1024)(128)(4,1)S(1)} %iota_compare_fusion.3) | copy-start | bytes 3076
  176.2 124.0 %all-gather.9.cloned.1.call-start = ((), (), s32[]{:S(2)}) async-start(), calls=%async_computation.18 | async-start | bytes 3932160 | tf_op jit(solution)/shard_map/all_gather | solution.py:246
  235.3 165.2 %reduce-scatter.23.cloned.1.call-start = ((), (), s32[]{:S(2)}) async-start(), calls=%async_computation.19 | async-start | bytes 3932160 | tf_op jit(solution)/shard_map/reduce_scatter | solution.py:277
  341.4 122.1 %reduce-scatter.15.cloned.1.call-start = ((), (), s32[]{:S(2)}) async-start(), calls=%async_computation.12 | async-start | bytes 3932160 | tf_op jit(solution)/shard_map/reduce_scatter | solution.py:198
  361.4 167.1 %copy-start.52 = (f32[768]{0:T(1024)S(1)}, f32[768]{0:T(1024)}, u32[]{:S(2)}) copy-start(f32[768]{0:T(1024)} %copy-done.51) | copy-start | bytes 9220
  361.5 167.1 %copy-start.54 = (f32[1024]{0:T(1024)S(1)}, f32[1024]{0:T(1024)}, u32[]{:S(2)}) copy-start(f32[1024]{0:T(1024)} %copy-done.53) | copy-start | bytes 12292
  361.5 167.1 %all-gather.11.cloned.1.call-start = ((), (), s32[]{:S(2)}) async-start(), calls=%async_computation.20 | async-start | bytes 3932160 | tf_op jit(solution)/shard_map/all_gather | solution.py:278
  400.4 131.2 %copy-start.58 = (f32[1024]{0:T(1024)S(1)}, f32[1024]{0:T(1024)}, u32[]{:S(2)}) copy-start(f32[1024]{0:T(1024)} %copy-done.57) | copy-start | bytes 12292
  400.5 191.9 %all-gather.5.cloned.1.call-start = ((), (), s32[]{:S(2)}) async-start(), calls=%async_computation.13 | async-start | bytes 3932160 | tf_op jit(solution)/shard_map/all_gather | solution.py:199
  463.5 203.8 %reduce-scatter.17.cloned.1.call-start = ((), (), s32[]{:S(2)}) async-start(), calls=%async_computation.14 | async-start | bytes 3932160 | tf_op jit(solution)/shard_map/reduce_scatter | solution.py:206
  531.6 68.0 %copy-start.28 = (bf16[768,512]{1,0:T(8,128)(2,1)S(1)}, bf16[768,512]{1,0:T(8,128)(2,1)}, u32[]{:S(2)}) copy-start(bf16[768,512]{1,0:T(8,128)(2,1)} %param.25) | copy-start | bytes 2359300
  531.6 67.9 %copy-start.50 = (f32[768]{0:T(1024)S(1)}, f32[768]{0:T(1024)}, u32[]{:S(2)}) copy-start(f32[768]{0:T(1024)} %copy-done.48) | copy-start | bytes 9220
  608.2 97.1 %reduce-scatter.37.cloned.1.call-start = ((), (), s32[]{:S(2)}) async-start(), calls=%async_computation.27 | async-start | bytes 884736
  612.8 134.9 %reduce-scatter.35.cloned.1.call-start = ((), (), s32[]{:S(2)}) async-start(), calls=%async_computation.26 | async-start | bytes 1769472 | tf_op jit(solution)/shard_map/reduce_scatter | solution.py:255
  618.5 171.4 %reduce-scatter.31.cloned.1.call-start = ((), (), s32[]{:S(2)}) async-start(), calls=%async_computation.24 | async-start | bytes 1769472 | tf_op jit(solution)/shard_map/reduce_scatter | solution.py:252
  621.0 211.3 %reduce-scatter.33.cloned.1.call-start = ((), (), s32[]{:S(2)}) async-start(), calls=%async_computation.25 | async-start | bytes 1769472 | tf_op jit(solution)/shard_map/reduce_scatter | solution.py:253
  625.1 245.8 %reduce-scatter.29.cloned.1.call-start = ((), (), s32[]{:S(2)}) async-start(), calls=%async_computation.23 | async-start | bytes 884736 | tf_op jit(solution)/shard_map/reduce_scatter | solution.py:286
  626.7 54.6 %copy-start.68 = (u32[32]{0:T(128)S(1)}, u32[32]{0:T(128)}, u32[]{:S(2)}) copy-start(u32[32]{0:T(128)} %constant.175) | copy-start | bytes 388
  626.7 59.8 %copy-start.26 = (bf16[1024,3,64]{0,2,1:T(8,128)(2,1)S(1)}, bf16[1024,3,64]{0,2,1:T(8,128)(2,1)}, u32[]{:S(2)}) copy-start(bf16[1024,3,64]{0,2,1:T(8,128)(2,1)} %copy-done.25) | copy-start | bytes 1179652
  626.7 282.7 %reduce-scatter.25.cloned.1.call-start = ((), (), s32[]{:S(2)}) async-start(), calls=%async_computation.21 | async-start | bytes 884736 | tf_op jit(solution)/shard_map/reduce_scatter | solution.py:284
  628.3 78.7 %copy-start.61 = (f32[768]{0:T(1024)S(1)}, f32[768]{0:T(1024)}, u32[]{:S(2)}) copy-start(f32[768]{0:T(1024)} %get-tuple-element.300) | copy-start | bytes 9220
  628.3 319.7 %reduce-scatter.27.cloned.1.call-start = ((), (), s32[]{:S(2)}) async-start(), calls=%async_computation.22 | async-start | bytes 884736 | tf_op jit(solution)/shard_map/reduce_scatter | solution.py:285
  668.7 12.6 %collective-permute-start = (bf16[256,768]{1,0:T(8,128)(2,1)S(1)}, bf16[256,768]{1,0:T(8,128)(2,1)S(1)}, u32[]{:S(2)}, u32[]{:S(2)}) collective-permute-start(bf16[256,768]{1,0:T(8,128)(2,1)S(1)} %select_convert_fusion), channel_id=1, source_target_pairs={{0,1},{1,2},{2,3},{3,0},{4,5},{5,6},{6,7},{7,4},{8,9},{9,10},{10,1... | collective-permute-start | bytes 1179656 | tf_op jit(solution)/shard_map/ppermute | solution.py:21
  681.3 39.4 %collective-permute-start.1 = (bf16[256,768]{1,0:T(8,128)(2,1)S(1)}, bf16[256,768]{1,0:T(8,128)(2,1)}, u32[]{:S(2)}, u32[]{:S(2)}) collective-permute-start(bf16[256,768]{1,0:T(8,128)(2,1)S(1)} %collective-permute-done), channel_id=1, source_target_pairs={{0,1},{1,2},{2,3},{3,0},{4,5},{5,6},{6,7},{7,4},{8,9},{9,10},{10,1... | collective-permute-start | bytes 1179656 | tf_op jit(solution)/shard_map/ppermute | solution.py:21
  682.5 39.3 %collective-permute-start.2 = (bf16[256,768]{1,0:T(8,128)(2,1)S(1)}, bf16[256,768]{1,0:T(8,128)(2,1)}, u32[]{:S(2)}, u32[]{:S(2)}) collective-permute-start(bf16[256,768]{1,0:T(8,128)(2,1)S(1)} %select_convert_fusion), channel_id=1, source_target_pairs={{0,3},{1,0},{2,1},{3,2},{4,7},{5,4},{6,5},{7,6},{8,11},{9,8},{10,9... | collective-permute-start | bytes 1179656 | tf_op jit(solution)/shard_map/ppermute | solution.py:23
  (69 other events, 172.4 us)
Sparse Core Ops, SparseCore 0:
  33.5 62.9 reduce-scatter.18
  98.1 63.5 all-gather.6
  176.3 58.8 reduce-scatter.20
  236.7 63.5 all-gather.8
  341.5 58.8 reduce-scatter.22
  403.2 60.2 reduce-scatter.14
  465.0 63.5 all-gather.10
  530.2 62.1 all-gather.4
  608.3 58.8 reduce-scatter.16
  670.2 35.0 reduce-scatter.36
  709.2 38.4 reduce-scatter.34
  751.4 38.4 reduce-scatter.30
  793.8 38.4 reduce-scatter.32
  835.8 34.9 reduce-scatter.28
  874.4 34.9 reduce-scatter.24
  913.0 34.9 reduce-scatter.26
